TPU v7x, 256 devices: a whole 4x4x8 slice. The times are simulated.
256 devices in a mesh: seq: 32 (over z, x_hi, core), head: 8 (over y, x_lo).
Axes of the slice: x: 4 (x_hi: 2, x_lo: 2; x = x_hi * 2 + x_lo), y: 4, z: 8, core: 2. Of those that a mesh axis runs over, the one named last changes fastest.
Arguments:
- queries: bfloat16 [6144, 4096], P('seq', 'head'), may hold values from -64 to 64
- key_one: bfloat16 [6144, 128], P('seq'), may hold values from -6 to 6
- key_two: bfloat16 [6144, 128], P('seq'), may hold values from -6 to 6
- value_one: bfloat16 [6144, 128], P('seq'), may hold values from -6 to 6
- value_two: bfloat16 [6144, 128], P('seq'), may hold values from -6 to 6
- residual_in: bfloat16 [6144, 4096], P(('seq', 'head')), may hold values from -6 to 6
- out_weight: bfloat16 [4096, 4096], P('head'), may hold values from -0.5 to 0.5
- norm_gain: float32 [4096], replicated, may hold values from 0.1 to 1.9
- gate_weight: bfloat16 [4096, 7168], P('seq', 'head'), may hold values from -0.09375 to 0.09375
- up_weight: bfloat16 [4096, 7168], P('seq', 'head'), may hold values from -0.09375 to 0.09375
Outputs:
- residual_out: bfloat16 [6144, 4096], P(('seq', 'head'))
- hidden: bfloat16 [6144, 7168], P('seq', 'head')
All inputs are finite; a program needn't handle non-finite values.
Results may differ from a plain program's by a relative error of at most 0.02.
Values may be sent and summed in bfloat16 or wider, within the bound.
No kernel may reach another device: no remote copies, remote signals or barrier semaphores. Data moves between devices by JAX's collectives and lax.ppermute only.
A program may use at most 64 MiB of HBM per device.

v0:
```python
import functools
import math

import jax
import jax.numpy as jnp
import numpy as np
from jax import lax
from jax.experimental import pallas as pl
from jax.experimental.pallas import tpu as pltpu
from jax.sharding import Mesh
from jax.sharding import PartitionSpec as P

LIMIT = 2.0 ** 90


def attention_kernel(heads, begin, stack, rank_ref, q_ref, far3_ref, far2_ref, far1_ref, own_ref, wo_ref, o_ref,
                     kt_ref, vx_ref, k2_ref, v2_ref, m_ref, acc_ref, weight_ref, sem):
    fetch = pltpu.make_async_copy(wo_ref, weight_ref, sem)
    fetch.start()
    count, width = q_ref.shape[0], kt_ref.shape[0]
    rows = own_ref.shape[0]
    groups = 8
    size, apart = count // groups, rows // groups
    span = 32
    third = far3_ref.shape[0]
    reach = third + 2 * rows
    total = reach + rows
    padded = kt_ref.shape[1]
    tile = 256
    rank = rank_ref[0]
    scale = 2.5 * width ** (-0.5) * math.log2(math.e)

    missing = jnp.maximum(reach - rows * rank, 0)
    k2_missing = jnp.where(rank == 0, span, 0)
    parts = [(far3_ref, 0, third), (far2_ref, third, rows), (far1_ref, third + rows, rows), (own_ref, reach, rows)]
    zero_pad = jnp.zeros((padded - total, width), jnp.bfloat16)
    keys = jnp.concatenate([ref[:, :width] for ref, _, _ in parts] + [zero_pad], axis=0)
    values = jnp.concatenate([ref[:, width:2 * width] for ref, _, _ in parts] + [zero_pad], axis=0)
    first = jnp.where(rank == 0, own_ref[0:16, :width].astype(jnp.float32),
             jnp.where(rank == 1, far1_ref[0:16, :width].astype(jnp.float32), far2_ref[0:16, :width].astype(jnp.float32)))[0:1]
    pos = lax.broadcasted_iota(jnp.int32, (padded, width), 0)
    absent = pos < missing
    keys = jnp.where(absent, jnp.broadcast_to(first, keys.shape), keys.astype(jnp.float32))
    kt_ref[...] = keys.T.astype(jnp.bfloat16)
    vx_ref[:, :width] = jnp.where(absent, 0.0, values.astype(jnp.float32)).astype(jnp.bfloat16)
    vx_ref[:, width:] = jnp.where(absent, 0.0, 1.0).astype(jnp.bfloat16)

    own2k = own_ref[:, 2 * width:3 * width].astype(jnp.float32)
    own2v = own_ref[:, 3 * width:4 * width].astype(jnp.float32)
    near2k = far1_ref[rows - span:, 2 * width:3 * width].astype(jnp.float32)
    near2v = far1_ref[rows - span:, 3 * width:4 * width].astype(jnp.float32)
    start = rank == 0
    k2 = jnp.concatenate([jnp.where(start, jnp.broadcast_to(own2k[0:1], near2k.shape), near2k), own2k], axis=0)
    v2 = jnp.concatenate([jnp.where(start, 0.0, near2v), own2v], axis=0)
    there = jnp.concatenate([jnp.where(start, 0.0, jnp.ones_like(near2v)), jnp.ones_like(own2v)], axis=0)
    for shift in range(8):
        kept = span + rows - shift
        k2_ref[shift, shift:] = k2[:kept]
        v2_ref[shift, shift:, :width] = v2[:kept]
        v2_ref[shift, shift:, width:] = there[:kept]

    def window(ref, offset):
        base = span + begin - offset // 8 * 8
        return jnp.concatenate([ref[offset % 8, pl.ds(pl.multiple_of(base + apart * g, 8), size), :] for g in range(groups)], axis=0)

    def at(shape):
        index = lax.broadcasted_iota(jnp.int32, shape, 0) % count
        return index // size * apart + index % size + begin

    def is_early(copies):
        shape = (copies * heads * count, tile)
        return lax.broadcasted_iota(jnp.int32, shape, 1) > at(shape)

    dot = functools.partial(jnp.dot, preferred_element_type=jnp.float32)

    def logits(offsets):
        pairs = []
        for offset in offsets:
            k2 = window(k2_ref, offset).astype(jnp.bfloat16)
            pairs += [q_ref[:, h * width:(h + 1) * width] * k2 for h in range(heads)]
        pair = jnp.concatenate(pairs, axis=0)
        return [dot(pair, kt_ref[:, i * tile:(i + 1) * tile]) for i in range(3)]

    def highest(offset):
        first, middle, last = logits([offset])
        return jnp.max(jnp.maximum(jnp.where(is_early(1), first, last), middle), axis=1, keepdims=True)

    def run():
        acc_ref[...] = jnp.zeros_like(acc_ref)

        def step(index, _):
            offsets = [index * stack + i for i in range(stack)]
            early = is_early(stack)
            first, middle, last = logits(offsets)
            m2 = jnp.concatenate([jnp.concatenate([m_ref[...]] * 2, axis=1)] * stack, axis=0)
            ends = jnp.exp2(jnp.where(early, first, last) * scale - m2)
            middle = jnp.exp2(middle * scale - m2).astype(jnp.bfloat16)
            p0 = jnp.where(early, ends, 0.0).astype(jnp.bfloat16)
            p2 = jnp.where(early, 0.0, ends).astype(jnp.bfloat16)
            r = dot(jnp.concatenate([p0, middle, p2], axis=1), vx_ref[...])
            for i, offset in enumerate(offsets):
                v2 = window(v2_ref, offset)
                for h in range(heads):
                    begins = (i * heads + h) * count
                    acc_ref[h * count:(h + 1) * count] += r[begins:begins + count] * v2
            return 0

        lax.fori_loop(0, span // stack, step, 0)

    m_ref[...] = jnp.broadcast_to(highest(0) * scale, m_ref.shape)
    run()
    worst = jnp.max(jnp.where(acc_ref[:, width:] < LIMIT, 0.0, 1.0))

    @pl.when(worst > 0.0)
    def _():
        def climb(offset, _):
            m_ref[...] = jnp.maximum(m_ref[...], jnp.broadcast_to(highest(offset) * scale, m_ref.shape))
            return 0

        lax.fori_loop(1, span, climb, 0)
        run()

    parts = []
    for h in range(heads):
        a = acc_ref[h * count:(h + 1) * count]
        parts.append((a[:, :width] / a[:, width:]).astype(jnp.bfloat16))
    attended = jnp.concatenate(parts, axis=1)
    fetch.wait()
    piece = 1024
    for at in range(0, o_ref.shape[1], piece):
        o_ref[:, at:at + piece] = dot(attended, weight_ref[:, at:at + piece]).astype(jnp.bfloat16)


def attend(queries, far3, far2, far1, own, rank, out_weight, begin, stack):
    count, cols = queries.shape
    rows, width = own.shape[0], own.shape[1] // 4
    heads = cols // width
    vm = pl.BlockSpec(memory_space=pltpu.VMEM)
    return pl.pallas_call(
        functools.partial(attention_kernel, heads, begin, stack),
        out_shape=jax.ShapeDtypeStruct((count, out_weight.shape[1]), jnp.bfloat16),
        in_specs=[pl.BlockSpec(memory_space=pltpu.SMEM)] + [vm] * 5 + [pl.BlockSpec(memory_space=pl.ANY)],
        out_specs=vm,
        scratch_shapes=[
            pltpu.VMEM((width, 768), jnp.bfloat16),
            pltpu.VMEM((768, 2 * width), jnp.bfloat16),
            pltpu.VMEM((8, rows + 32, width), jnp.float32),
            pltpu.VMEM((8, rows + 32, 2 * width), jnp.float32),
            pltpu.VMEM((heads * count, width), jnp.float32),
            pltpu.VMEM((heads * count, 2 * width), jnp.float32),
            pltpu.VMEM(out_weight.shape, jnp.bfloat16),
            pltpu.SemaphoreType.DMA,
        ],
        compiler_params=pltpu.CompilerParams(vmem_limit_bytes=48 * 2**20),
        cost_estimate=pl.CostEstimate(
            flops=count * heads * 32 * 1536 * 512, bytes_accessed=6_000_000, transcendentals=count * heads * 32 * 512
        ),
        name="attention",
    )(rank, queries, far3, far2, far1, own, out_weight)


SEQ = ("z", "xh", "core")
HEAD = ("y", "xl")


def prepare_kernel(core_ref, k1_ref, v1_ref, k2_ref, v2_ref, gate_ref, up_ref, own_ref, far_ref, last_ref, kept_ref, sent_ref):
    width = k1_ref.shape[1]
    skipped = k1_ref.shape[0] - last_ref.shape[0]
    for at, ref in enumerate((k1_ref, v1_ref, k2_ref, v2_ref)):
        own_ref[:, at * width : (at + 1) * width] = ref[...]
        if at < 2:
            far_ref[:, at * width : (at + 1) * width] = ref[...]
            last_ref[:, at * width : (at + 1) * width] = ref[skipped:, :]

    @pl.when(core_ref[0] == 0)
    def _():
        kept_ref[...] = gate_ref[...]
        sent_ref[...] = up_ref[...]

    @pl.when(core_ref[0] != 0)
    def _():
        kept_ref[...] = up_ref[...]
        sent_ref[...] = gate_ref[...]


def prepare(core, key_one, value_one, key_two, value_two, gate_weight, up_weight, last):
    rows, width = key_one.shape
    shape = lambda *dims: jax.ShapeDtypeStruct(dims, jnp.bfloat16)
    return pl.pallas_call(
        prepare_kernel,
        out_shape=(
            shape(rows, 4 * width),
            shape(rows, 2 * width),
            shape(last, 2 * width),
            shape(*gate_weight.shape),
            shape(*gate_weight.shape),
        ),
        in_specs=[pl.BlockSpec(memory_space=pltpu.SMEM)] + [pl.BlockSpec()] * 6,
        out_specs=(pl.BlockSpec(memory_space=pltpu.VMEM),) * 5,
        compiler_params=pltpu.CompilerParams(vmem_limit_bytes=60 * 2**20),
        name="prepare",
    )(core, key_one, value_one, key_two, value_two, gate_weight, up_weight)


def product_kernel(place_ref, ours_ref, theirs_ref, near_ref, far_ref, us_ref, them_ref, w_ref, total_ref, sems):
    chunks, block, _ = w_ref.shape
    rows, half = us_ref.shape[0], block // 2
    planes = chunks // 2
    cross, core = place_ref[0], place_ref[1]
    sources = [(near_ref, plane) for plane in range(planes)] + [(far_ref, plane) for plane in range(planes)]
    copies = [
        pltpu.make_async_copy(ref.at[pl.ds(plane * block, block), :], w_ref.at[i], sems.at[i])
        for i, (ref, plane) in enumerate(sources)
    ]
    for copy in copies:
        copy.start()
    together = 4
    for first in range(0, chunks, together):
        columns = []
        for i in range(first, first + together):
            copies[i].wait()
            plane = i % planes
            side = cross if i < planes else 1 - cross
            for part in (core, 1 - core):
                at = pl.multiple_of(((plane * 2 + side) * 2 + part) * half, half)
                columns.append(
                    jnp.concatenate([ours_ref[:, pl.ds(at, half)], theirs_ref[:, pl.ds(at, half)]], axis=0)
                )
        x = jnp.concatenate(columns, axis=1)
        w = w_ref[first : first + together].reshape(together * block, w_ref.shape[2])
        part = jnp.dot(x, w, preferred_element_type=jnp.float32)
        if first == 0:
            total_ref[...] = part
        else:
            total_ref[...] += part
    us_ref[...] = total_ref[:rows]
    them_ref[...] = total_ref[rows:].astype(jnp.bfloat16)


def product(place, ours, theirs, near, far):
    rows, depth = ours.shape
    width, block = near.shape[1], 256
    vm, hbm = pl.BlockSpec(memory_space=pltpu.VMEM), pl.BlockSpec(memory_space=pl.ANY)
    return pl.pallas_call(
        product_kernel,
        out_shape=(jax.ShapeDtypeStruct((rows, width), jnp.float32), jax.ShapeDtypeStruct((rows, width), jnp.bfloat16)),
        in_specs=[pl.BlockSpec(memory_space=pltpu.SMEM), vm, vm, hbm, hbm],
        out_specs=(vm, vm),
        scratch_shapes=[
            pltpu.VMEM((depth // block, block, width), jnp.bfloat16),
            pltpu.VMEM((2 * rows, width), jnp.float32),
            pltpu.SemaphoreType.DMA((depth // block,)),
        ],
        compiler_params=pltpu.CompilerParams(vmem_limit_bytes=48 * 2**20),
        cost_estimate=pl.CostEstimate(
            flops=4 * rows * depth * width, bytes_accessed=2 * depth * (2 * rows + width), transcendentals=0
        ),
        name="product",
    )(place, ours, theirs, near, far)


def finish_kernel(place_ref, us_ref, back_ref, o_ref):
    def store(gate, up):
        o_ref[...] = (gate / (1.0 + jnp.exp(-gate)) * up).astype(jnp.bfloat16)

    @pl.when(place_ref[1] == 0)
    def _():
        store(us_ref[...], back_ref[...].astype(jnp.float32))

    @pl.when(place_ref[1] != 0)
    def _():
        store(back_ref[...].astype(jnp.float32), us_ref[...])


def finish(place, for_us, back):
    vm = pl.BlockSpec(memory_space=pltpu.VMEM)
    return pl.pallas_call(
        finish_kernel,
        out_shape=jax.ShapeDtypeStruct(back.shape, jnp.bfloat16),
        in_specs=[pl.BlockSpec(memory_space=pltpu.SMEM), vm, vm],
        out_specs=vm,
        compiler_params=pltpu.CompilerParams(vmem_limit_bytes=48 * 2**20),
        name="finish",
    )(place, for_us, back)


def swapped(block, axis):
    return lax.ppermute(block, axis, [(0, 1), (1, 0)])


def from_behind(block, distance):
    devices = range(lax.axis_size(SEQ))
    route = [(i - distance, i) for i in devices if i - distance in devices]
    return lax.ppermute(block, SEQ, route)


def over_heads(tiles):
    return lax.all_to_all(tiles, HEAD, 0, 0, tiled=True)


def normalize(summed, norm_gain):
    mean_square = jnp.mean(summed * summed, axis=1, keepdims=True)
    scaled = summed * lax.rsqrt(mean_square + 1e-05) * norm_gain
    return scaled.astype(jnp.bfloat16)


def body(queries, key_one, key_two, value_one, value_two, residual_in, out_weight, norm_gain, gate_weight, up_weight):
    rows, _ = queries.shape
    peers = lax.axis_size(HEAD)
    core = lax.axis_index("core").astype(jnp.int32)
    own, far, last, kept, sent = prepare(
        core.reshape(1), key_one, value_one, key_two, value_two, gate_weight, up_weight, 512 - 2 * rows
    )
    mine = jnp.concatenate([kept, swapped(sent, "core")], axis=0)
    near = lax.all_gather(mine, "z", axis=0, tiled=True)
    other = swapped(mine, "xh")
    place = jnp.stack([lax.axis_index("xh").astype(jnp.int32), core])
    rank = lax.axis_index(SEQ).astype(jnp.int32).reshape(1)
    far1 = from_behind(own, 1)
    far2 = from_behind(far, 2)
    far3 = from_behind(last, 3)
    far_weight = lax.all_gather(other, "z", axis=0, tiled=True)
    partial = attend(queries, far3, far2, far1, own, rank, out_weight, 0, 1)
    arrived = over_heads(partial.reshape(peers, rows // peers, -1)).astype(jnp.float32).sum(axis=0)
    summed = residual_in.astype(jnp.float32) + arrived
    residual_out = summed.astype(jnp.bfloat16)
    own_rows = normalize(summed, norm_gain)
    ours = over_heads(jnp.broadcast_to(own_rows[None], (peers, *own_rows.shape))).reshape(rows, -1)
    theirs = swapped(ours, "core")
    for_us, for_them = product(place, ours, theirs, near, far_weight)
    hidden = finish(place, for_us, swapped(for_them, "core"))
    return (residual_out, hidden)


def solution(mesh):
    fine = Mesh(np.asarray(mesh.devices).reshape(8, 2, 2, 4, 2), SEQ + HEAD)
    return jax.shard_map(
        body,
        mesh=fine,
        in_specs=(
            P(SEQ, HEAD),
            P(SEQ, None),
            P(SEQ, None),
            P(SEQ, None),
            P(SEQ, None),
            P(SEQ + HEAD, None),
            P(HEAD, None),
            P(),
            P(SEQ, HEAD),
            P(SEQ, HEAD),
        ),
        out_specs=(P(SEQ + HEAD, None), P(SEQ, HEAD)),
        check_vma=False,
    )
```

profile of v0, /device:TPU:1, one launch (start us, length us, event | category | flops | bytes accessed | tf_op | source)
XLA Modules:
  0.0 134.1 jit_solution(17282642392949077974)
XLA Ops:
  7.2 0.0 all-gather.3.cloned.1.call-start
  7.2 2.2 %prepare.1 = (bf16[192,512]{1,0:T(8,128)(2,1)}, bf16[192,256]{1,0:T(8,128)(2,1)}, bf16[128,256]{1,0:T(8,128)(2,1)}, bf16[128,896]{1,0:T(8,128)(2,1)}, bf16[128,896]{1,0:T(8,128)(2,1)}) custom-call(s32[1]{0:T(128)} %bitcast.1.core_ref, bf16[192,128]{1,0:T(8,128)(2,1)} %k1_ref.1, bf16[192,128]{1,0:T(8,128)(2,1)} %v1_ref.1, bf16[192,128]{1,0:T(8,128)(2,1)} %k2_ref.1, ...), custom_call_target="tpu_custom_call" | custom-call | tf_op jit(solution)/shard_map/prepare/pallas_call | solution.py:189
  9.4 3.2 %collective-permute-start.4 = (bf16[128,896]{1,0:T(8,128)(2,1)}, bf16[128,896]{1,0:T(8,128)(2,1)S(1)}, u32[]{:S(2)}, u32[]{:S(2)}) collective-permute-start(bf16[128,896]{1,0:T(8,128)(2,1)} %get-tuple-element.13), channel_id=1, source_target_pairs={{0,8},{8,0},{1,9},{9,1},{2,10},{10,2},{3,11},{11,3},{4,12},{12,4},... | collective-permute-start | bytes 688136 | tf_op jit(solution)/shard_map/ppermute | solution.py:288
  12.6 1.0 constant_dynamic-update-slice_fusion.1
  13.6 0.4 collective-permute-done.4
  14.0 0.8 copy-done.2
  14.7 0.0 all-gather.3.cloned.1.call-update
  14.7 0.0 all-gather.5.cloned.1.call-start
  14.8 1.1 collective-permute-start.5
  15.9 4.4 %collective-permute-start.2 = (bf16[192,512]{1,0:T(8,128)(2,1)}, bf16[192,512]{1,0:T(8,128)(2,1)S(1)}, u32[]{:S(2)}, u32[]{:S(2)}) collective-permute-start(bf16[192,512]{1,0:T(8,128)(2,1)} %get-tuple-element.11.own_ref), channel_id=1, source_target_pairs={{0,8},{8,16},{16,24},{24,32},{32,40},{40,48},{48,56},{56,64},{64,7... | collective-permute-start | bytes 589832 | tf_op jit(solution)/shard_map/ppermute | solution.py:294
  20.3 4.3 %collective-permute-start.1 = (bf16[192,256]{1,0:T(8,128)(2,1)}, bf16[192,256]{1,0:T(8,128)(2,1)S(1)}, u32[]{:S(2)}, u32[]{:S(2)}) collective-permute-start(bf16[192,256]{1,0:T(8,128)(2,1)} %get-tuple-element.10), channel_id=1, source_target_pairs={{0,16},{8,24},{16,32},{24,40},{32,48},{40,56},{48,64},{56,72},{64,... | collective-permute-start | bytes 294920 | tf_op jit(solution)/shard_map/ppermute | solution.py:294
  24.6 1.3 collective-permute-start
  25.9 2.4 %collective-permute-done.5 = bf16[256,896]{1,0:T(8,128)(2,1)S(1)} collective-permute-done((bf16[256,896]{1,0:T(8,128)(2,1)}, bf16[256,896]{1,0:T(8,128)(2,1)S(1)}, u32[]{:S(2)}, u32[]{:S(2)}) %collective-permute-start.5) | collective-permute-done | bytes 458784 | tf_op jit(solution)/shard_map/ppermute | solution.py:288
  28.3 0.8 copy-done.4
  29.1 0.0 all-gather.5.cloned.1.call-update
  29.2 2.3 %collective-permute-done.1.far2_ref = bf16[192,256]{1,0:T(8,128)(2,1)S(1)} collective-permute-done((bf16[192,256]{1,0:T(8,128)(2,1)}, bf16[192,256]{1,0:T(8,128)(2,1)S(1)}, u32[]{:S(2)}, u32[]{:S(2)}) %collective-permute-start.1) | collective-permute-done | bytes 98336 | tf_op jit(solution)/shard_map/ppermute | solution.py:294
  31.5 27.3 %attention.1 = bf16[192,4096]{1,0:T(8,128)(2,1)S(1)} custom-call(s32[1]{0:T(128)} %bitcast.rank_ref, bf16[192,512]{1,0:T(8,128)(2,1)S(1)} %copy-done, bf16[128,256]{1,0:T(8,128)(2,1)S(1)} %collective-permute-done.far3_ref, bf16[192,256]{1,0:T(8,128)(2,1)S(1)} %collective-permute-done.1.far2_ref, bf16[192,512]{1,0:T(8,128)(2,1)S(1)} %collective-permute-done.2.far1_ref, ...), custom_call_target="tpu_custom_call" | custom-call | flops 19327352832 | bytes 6000000 | tf_op jit(solution)/shard_map/attention/pallas_call | solution.py:139
  58.8 25.3 %all_to_all.10 = bf16[8,24,4096]{2,1,0:T(8,128)(2,1)S(1)} all-to-all(bf16[8,24,4096]{2,1,0:T(8,128)(2,1)S(1)} %bitcast.7), channel_id=1, replica_groups=mesh['z'=8,'xh'=2,'core'=2,'y'=4,'xl'=2] {'y','xl'}, dimensions={0} | all-to-all | bytes 3145728 | tf_op jit(solution)/shard_map/all_to_all | solution.py:298
  84.1 0.2 convert_reduce_fusion
  84.3 0.7 copy-done.3
  85.0 0.2 multiply_reduce_fusion
  85.2 0.7 multiply_convert_fusion
  85.9 0.2 broadcast_in_dim.2
  86.1 23.2 %all_to_all.11 = bf16[8,24,4096]{2,1,0:T(8,128)(2,1)S(1)} all-to-all(bf16[8,24,4096]{2,1,0:T(8,128)(2,1)S(1)} %broadcast_in_dim.2), channel_id=1, replica_groups=mesh['z'=8,'xh'=2,'core'=2,'y'=4,'xl'=2] {'y','xl'}, dimensions={0} | all-to-all | bytes 3145728 | tf_op jit(solution)/shard_map/all_to_all | solution.py:298
  109.3 1.8 %collective-permute-start.3 = (bf16[192,4096]{1,0:T(8,128)(2,1)S(1)}, bf16[192,4096]{1,0:T(8,128)(2,1)S(1)}, u32[]{:S(2)}, u32[]{:S(2)}) collective-permute-start(bf16[192,4096]{1,0:T(8,128)(2,1)S(1)} %bitcast.5), channel_id=1, source_target_pairs={{0,8},{8,0},{1,9},{9,1},{2,10},{10,2},{3,11},{11,3},{4,12},{12,4},... | collective-permute-start | bytes 4718600 | tf_op jit(solution)/shard_map/ppermute | solution.py:288
  111.2 0.1 pad_add_fusion.place_ref
  111.3 3.0 %collective-permute-done.3.theirs_ref = bf16[192,4096]{1,0:T(8,128)(2,1)S(1)} collective-permute-done((bf16[192,4096]{1,0:T(8,128)(2,1)S(1)}, bf16[192,4096]{1,0:T(8,128)(2,1)S(1)}, u32[]{:S(2)}, u32[]{:S(2)}) %collective-permute-start.3) | collective-permute-done | bytes 1572896 | tf_op jit(solution)/shard_map/ppermute | solution.py:288
  114.2 3.1 %all-gather.5.cloned.1.call-done.far_ref = bf16[2048,896]{1,0:T(8,128)(2,1)} async-done(((bf16[256,896]{1,0:T(8,128)(2,1)}), bf16[2048,896]{1,0:T(8,128)(2,1)}) %all-gather.5.cloned.1.call-update) | async-done | bytes 3670032 | tf_op jit(solution)/shard_map/all_gather | solution.py:322
  117.3 6.2 %product.1 = (f32[192,896]{1,0:T(8,128)S(1)}, bf16[192,896]{1,0:T(8,128)(2,1)S(1)}) custom-call(s32[2]{0:T(128)S(1)} %pad_add_fusion.place_ref, bf16[192,4096]{1,0:T(8,128)(2,1)S(1)} %bitcast.6, bf16[192,4096]{1,0:T(8,128)(2,1)S(1)} %collective-permute-done.3.theirs_ref, bf16[2048,896]{1,0:T(8,128)(2,1)} %all-gather.3.cloned.1.call-done.near_ref, ...), custom_call_target="tpu_custom_call" | custom-call | flops 2818572288 | bytes 10485760 | tf_op jit(solution)/shard_map/product/pallas_call | solution.py:244
  123.5 0.9 collective-permute-start.6
  124.5 1.3 collective-permute-done.6.back_ref
  125.7 1.5 %finish.1 = bf16[192,896]{1,0:T(8,128)(2,1)} custom-call(s32[2]{0:T(128)S(1)} %pad_add_fusion.place_ref, f32[192,896]{1,0:T(8,128)S(1)} %get-tuple-element.14.us_ref, bf16[192,896]{1,0:T(8,128)(2,1)S(1)} %collective-permute-done.6.back_ref), custom_call_target="tpu_custom_call" | custom-call | tf_op jit(solution)/shard_map/finish/pallas_call | solution.py:277
  (14 shorter events, 0.1 us)
Async XLA Ops:
  7.2 24.3 %copy-start = (bf16[192,512]{1,0:T(8,128)(2,1)S(1)}, bf16[192,512]{1,0:T(8,128)(2,1)}, u32[]{:S(2)}) copy-start(bf16[192,512]{1,0:T(8,128)(2,1)} %q_ref.1) | copy-start | bytes 589828
  7.2 107.1 %all-gather.3.cloned.1.call-start = ((), (), s32[]{:S(2)}) async-start(), calls=%async_computation.2 | async-start | bytes 4128768 | tf_op jit(solution)/shard_map/all_gather | solution.py:315
  9.4 22.1 %copy-start.1 = (bf16[192,512]{1,0:T(8,128)(2,1)S(1)}, bf16[192,512]{1,0:T(8,128)(2,1)}, u32[]{:S(2)}) copy-start(bf16[192,512]{1,0:T(8,128)(2,1)} %get-tuple-element.11.own_ref) | copy-start | bytes 589828
  9.4 4.5 %collective-permute-start.4 = (bf16[128,896]{1,0:T(8,128)(2,1)}, bf16[128,896]{1,0:T(8,128)(2,1)S(1)}, u32[]{:S(2)}, u32[]{:S(2)}) collective-permute-start(bf16[128,896]{1,0:T(8,128)(2,1)} %get-tuple-element.13), channel_id=1, source_target_pairs={{0,8},{8,0},{1,9},{9,1},{2,10},{10,2},{3,11},{11,3},{4,12},{12,4},... | collective-permute-start | bytes 688136 | tf_op jit(solution)/shard_map/ppermute | solution.py:288
  13.9 0.8 copy-start.2
  14.7 102.6 %all-gather.5.cloned.1.call-start = ((), (), s32[]{:S(2)}) async-start(), calls=%async_computation.3 | async-start | bytes 4128768 | tf_op jit(solution)/shard_map/all_gather | solution.py:322
  14.8 13.5 %collective-permute-start.5 = (bf16[256,896]{1,0:T(8,128)(2,1)}, bf16[256,896]{1,0:T(8,128)(2,1)S(1)}, u32[]{:S(2)}, u32[]{:S(2)}) collective-permute-start(bf16[256,896]{1,0:T(8,128)(2,1)} %copy-done.2), channel_id=1, source_target_pairs={{0,16},{16,0},{1,17},{17,1},{2,18},{18,2},{3,19},{19,3},{4,20},{20... | collective-permute-start | bytes 1376264 | tf_op jit(solution)/shard_map/ppermute | solution.py:288
  15.9 15.6 %collective-permute-start.2 = (bf16[192,512]{1,0:T(8,128)(2,1)}, bf16[192,512]{1,0:T(8,128)(2,1)S(1)}, u32[]{:S(2)}, u32[]{:S(2)}) collective-permute-start(bf16[192,512]{1,0:T(8,128)(2,1)} %get-tuple-element.11.own_ref), channel_id=1, source_target_pairs={{0,8},{8,16},{16,24},{24,32},{32,40},{40,48},{48,56},{56,64},{64,7... | collective-permute-start | bytes 589832 | tf_op jit(solution)/shard_map/ppermute | solution.py:294
  20.3 11.2 %collective-permute-start.1 = (bf16[192,256]{1,0:T(8,128)(2,1)}, bf16[192,256]{1,0:T(8,128)(2,1)S(1)}, u32[]{:S(2)}, u32[]{:S(2)}) collective-permute-start(bf16[192,256]{1,0:T(8,128)(2,1)} %get-tuple-element.10), channel_id=1, source_target_pairs={{0,16},{8,24},{16,32},{24,40},{32,48},{40,56},{48,64},{56,72},{64,... | collective-permute-start | bytes 294920 | tf_op jit(solution)/shard_map/ppermute | solution.py:294
  24.6 4.6 %collective-permute-start = (bf16[128,256]{1,0:T(8,128)(2,1)}, bf16[128,256]{1,0:T(8,128)(2,1)S(1)}, u32[]{:S(2)}, u32[]{:S(2)}) collective-permute-start(bf16[128,256]{1,0:T(8,128)(2,1)} %get-tuple-element.9), channel_id=1, source_target_pairs={{0,24},{8,32},{16,40},{24,48},{32,56},{40,64},{48,72},{56,80},{64,... | collective-permute-start | bytes 196616 | tf_op jit(solution)/shard_map/ppermute | solution.py:294
  28.3 0.8 copy-start.4
  84.1 0.9 copy-start.3
  84.1 1.1 copy-start.5
  109.3 4.9 %collective-permute-start.3 = (bf16[192,4096]{1,0:T(8,128)(2,1)S(1)}, bf16[192,4096]{1,0:T(8,128)(2,1)S(1)}, u32[]{:S(2)}, u32[]{:S(2)}) collective-permute-start(bf16[192,4096]{1,0:T(8,128)(2,1)S(1)} %bitcast.5), channel_id=1, source_target_pairs={{0,8},{8,0},{1,9},{9,1},{2,10},{10,2},{3,11},{11,3},{4,12},{12,4},... | collective-permute-start | bytes 4718600 | tf_op jit(solution)/shard_map/ppermute | solution.py:288
  123.5 2.2 %collective-permute-start.6 = (bf16[192,896]{1,0:T(8,128)(2,1)S(1)}, bf16[192,896]{1,0:T(8,128)(2,1)S(1)}, u32[]{:S(2)}, u32[]{:S(2)}) collective-permute-start(bf16[192,896]{1,0:T(8,128)(2,1)S(1)} %get-tuple-element.15), channel_id=1, source_target_pairs={{0,8},{8,0},{1,9},{9,1},{2,10},{10,2},{3,11},{11,3},{4,12},{12,4},... | collective-permute-start | bytes 1032200 | tf_op jit(solution)/shard_map/ppermute | solution.py:288
Sparse Core Ops, SparseCore 0:
  14.9 50.3 all-gather.2
  67.0 50.2 all-gather.4
where the time goes:
time: 134 us
  blocking collectives  48.6 us (36%)
  Pallas kernels  37.1 us (28%)
  starting transfers between devices  17.1 us (13%)
  between operations  14.2 us (11%)
  waiting for transfers between devices  12.5 us (9%)
  local copies, waits for them, and re-layouts  3.47 us (3%)
    all_to_all x2, blocking collectives, over_heads(): return lax.all_to_all(tiles, HEAD, 0, 0, tiled=True)  48.6 us
    pallas_call x1, Pallas kernels, attend(): pl.pallas_call(functools.partial(attention_kernel, heads, begin, stack),...  27.3 us
    ppermute x3, starting transfers between devices, from_behind(): return lax.ppermute(block, SEQ, route)  9.96 us
    ppermute x4, starting transfers between devices, swapped(): return lax.ppermute(block, axis, [(0, 1), (1, 0)])  7.1 us
    ppermute x4, waiting for transfers between devices, swapped(): return lax.ppermute(block, axis, [(0, 1), (1, 0)])  6.99 us
    pallas_call x1, Pallas kernels, product(): pl.pallas_call(product_kernel, out_shape=(jax.ShapeDtypeStruct((rows, wid...  6.17 us
    unnamed x13, local copies, waits for them, and re-layouts  3.28 us
    all_gather x1, waiting for transfers between devices, body(): far_weight = lax.all_gather(other, 'z', axis=0, tiled=True)  3.11 us
  transfers between devices with their start and end apart: 9, of which 6 were waited for; matrix products, arithmetic and copies ran while one was open for 2% of the time, Pallas kernels for 20%

commit v1 on v0

--- a/solution.py
+++ b/solution.py
@@ -298,10 +298,35 @@
     return lax.all_to_all(tiles, HEAD, 0, 0, tiled=True)
 
 
-def normalize(summed, norm_gain):
-    mean_square = jnp.mean(summed * summed, axis=1, keepdims=True)
-    scaled = summed * lax.rsqrt(mean_square + 1e-05) * norm_gain
-    return scaled.astype(jnp.bfloat16)
+def norm_kernel(arrived_ref, residual_ref, gain_ref, residual_out_ref, tiles_ref):
+    peers, rows, cols = arrived_ref.shape
+    gain = gain_ref[...]
+    for at in range(0, rows, 8):
+        part = pl.ds(at, 8)
+        total = arrived_ref[0, part, :].astype(jnp.float32)
+        for i in range(1, peers):
+            total += arrived_ref[i, part, :].astype(jnp.float32)
+        summed = residual_ref[part, :].astype(jnp.float32) + total
+        residual_out_ref[part, :] = summed.astype(jnp.bfloat16)
+        mean_square = jnp.sum(summed * summed, axis=1, keepdims=True) / cols
+        normed = (summed * lax.rsqrt(mean_square + 1e-05) * gain).astype(jnp.bfloat16)
+        for i in range(peers):
+            tiles_ref[i, part, :] = normed
+
+
+def normalize(arrived, residual_in, norm_gain):
+    vm = pl.BlockSpec(memory_space=pltpu.VMEM)
+    return pl.pallas_call(
+        norm_kernel,
+        out_shape=(
+            jax.ShapeDtypeStruct(residual_in.shape, jnp.bfloat16),
+            jax.ShapeDtypeStruct(arrived.shape, jnp.bfloat16),
+        ),
+        in_specs=[vm, vm, vm],
+        out_specs=(vm, vm),
+        compiler_params=pltpu.CompilerParams(vmem_limit_bytes=24 * 2**20),
+        name="normalize",
+    )(arrived, residual_in, norm_gain.reshape(1, -1))
 
 
 def body(queries, key_one, key_two, value_one, value_two, residual_in, out_weight, norm_gain, gate_weight, up_weight):
@@ -321,11 +346,9 @@
     far3 = from_behind(last, 3)
     far_weight = lax.all_gather(other, "z", axis=0, tiled=True)
     partial = attend(queries, far3, far2, far1, own, rank, out_weight, 0, 1)
-    arrived = over_heads(partial.reshape(peers, rows // peers, -1)).astype(jnp.float32).sum(axis=0)
-    summed = residual_in.astype(jnp.float32) + arrived
-    residual_out = summed.astype(jnp.bfloat16)
-    own_rows = normalize(summed, norm_gain)
-    ours = over_heads(jnp.broadcast_to(own_rows[None], (peers, *own_rows.shape))).reshape(rows, -1)
+    arrived = over_heads(partial.reshape(peers, rows // peers, -1))
+    residual_out, tiles = normalize(arrived, residual_in, norm_gain)
+    ours = over_heads(tiles).reshape(rows, -1)
     theirs = swapped(ours, "core")
     for_us, for_them = product(place, ours, theirs, near, far_weight)
     hidden = finish(place, for_us, swapped(for_them, "core"))

time: 134 us -> 146 us (1.090)
  the two profiles are of different devices: /device:TPU:1 before, /device:TPU:100 now
where the time goes in v1:
time: 146 us
  blocking collectives  52.4 us (36%)
  Pallas kernels  38.1 us (26%)
  waiting for transfers between devices  25.3 us (17%)
  between operations  14.2 us (10%)
  starting transfers between devices  13.2 us (9%)
  local copies, waits for them, and re-layouts  2.65 us (2%)
    all_to_all x2, blocking collectives, over_heads(): return lax.all_to_all(tiles, HEAD, 0, 0, tiled=True)  52.4 us
    pallas_call x1, Pallas kernels, attend(): pl.pallas_call(functools.partial(attention_kernel, heads, begin, stack),...  27.3 us
    ppermute x4, waiting for transfers between devices, swapped(): return lax.ppermute(block, axis, [(0, 1), (1, 0)])  19.3 us
    ppermute x3, starting transfers between devices, from_behind(): return lax.ppermute(block, SEQ, route)  12.2 us
    pallas_call x1, Pallas kernels, product(): pl.pallas_call(product_kernel, out_shape=(jax.ShapeDtypeStruct((rows, wid...  6.17 us
    ppermute x3, waiting for transfers between devices, from_behind(): return lax.ppermute(block, SEQ, route)  6.02 us
  transfers between devices with their start and end apart: 9, of which 5 were waited for; matrix products, arithmetic and copies ran while one was open for 1% of the time, Pallas kernels for 19%

profile of v1, /device:TPU:100, one launch (start us, length us, event | category | flops | bytes accessed | tf_op | source)
XLA Modules:
  0.0 145.9 jit_solution(12715347276918045900)
XLA Ops:
  7.2 0.0 all-gather.3.cloned.1.call-start
  7.2 2.2 %prepare.1 = (bf16[192,512]{1,0:T(8,128)(2,1)}, bf16[192,256]{1,0:T(8,128)(2,1)}, bf16[128,256]{1,0:T(8,128)(2,1)}, bf16[128,896]{1,0:T(8,128)(2,1)}, bf16[128,896]{1,0:T(8,128)(2,1)}) custom-call(s32[1]{0:T(128)} %bitcast.1.core_ref, bf16[192,128]{1,0:T(8,128)(2,1)} %k1_ref.1, bf16[192,128]{1,0:T(8,128)(2,1)} %v1_ref.1, bf16[192,128]{1,0:T(8,128)(2,1)} %k2_ref.1, ...), custom_call_target="tpu_custom_call" | custom-call | tf_op jit(solution)/shard_map/prepare/pallas_call | solution.py:189
  9.4 0.1 collective-permute-start.4
  9.5 1.0 constant_dynamic-update-slice_fusion.1
  10.5 0.7 collective-permute-done.4
  11.2 0.0 copy-start.4
  11.2 0.8 copy-done.4
  12.0 0.0 all-gather.3.cloned.1.call-update
  12.0 0.0 all-gather.5.cloned.1.call-start
  12.0 0.6 collective-permute-start.5
  12.6 13.8 %collective-permute-done.5 = bf16[256,896]{1,0:T(8,128)(2,1)S(1)} collective-permute-done((bf16[256,896]{1,0:T(8,128)(2,1)}, bf16[256,896]{1,0:T(8,128)(2,1)S(1)}, u32[]{:S(2)}, u32[]{:S(2)}) %collective-permute-start.5) | collective-permute-done | bytes 458784 | tf_op jit(solution)/shard_map/ppermute | solution.py:288
  26.4 0.8 copy-done.5
  27.2 0.0 all-gather.5.cloned.1.call-update
  27.3 1.9 %collective-permute-start.2 = (bf16[192,512]{1,0:T(8,128)(2,1)S(1)}, bf16[192,512]{1,0:T(8,128)(2,1)S(1)}, u32[]{:S(2)}, u32[]{:S(2)}) collective-permute-start(bf16[192,512]{1,0:T(8,128)(2,1)S(1)} %copy-done.3), channel_id=1, source_target_pairs={{0,8},{8,16},{16,24},{24,32},{32,40},{40,48},{48,56},{56,64},{64,7... | collective-permute-start | bytes 589832 | tf_op jit(solution)/shard_map/ppermute | solution.py:294
  29.2 5.0 %collective-permute-start.1 = (bf16[192,256]{1,0:T(8,128)(2,1)S(1)}, bf16[192,256]{1,0:T(8,128)(2,1)S(1)}, u32[]{:S(2)}, u32[]{:S(2)}) collective-permute-start(bf16[192,256]{1,0:T(8,128)(2,1)S(1)} %copy-done.6), channel_id=1, source_target_pairs={{0,16},{8,24},{16,32},{24,40},{32,48},{40,56},{48,64},{56,72},{64,... | collective-permute-start | bytes 294920 | tf_op jit(solution)/shard_map/ppermute | solution.py:294
  34.2 5.3 %collective-permute-start = (bf16[128,256]{1,0:T(8,128)(2,1)S(1)}, bf16[128,256]{1,0:T(8,128)(2,1)S(1)}, u32[]{:S(2)}, u32[]{:S(2)}) collective-permute-start(bf16[128,256]{1,0:T(8,128)(2,1)S(1)} %copy-done.7), channel_id=1, source_target_pairs={{0,24},{8,32},{16,40},{24,48},{32,56},{40,64},{48,72},{56,80},{64,... | collective-permute-start | bytes 196616 | tf_op jit(solution)/shard_map/ppermute | solution.py:294
  39.5 6.0 %collective-permute-done.far3_ref = bf16[128,256]{1,0:T(8,128)(2,1)S(1)} collective-permute-done((bf16[128,256]{1,0:T(8,128)(2,1)S(1)}, bf16[128,256]{1,0:T(8,128)(2,1)S(1)}, u32[]{:S(2)}, u32[]{:S(2)}) %collective-permute-start) | collective-permute-done | bytes 65568 | tf_op jit(solution)/shard_map/ppermute | solution.py:294
  45.6 0.0 collective-permute-done.1.far2_ref
  45.6 0.0 collective-permute-done.2.far1_ref
  45.6 27.3 %attention.1 = bf16[192,4096]{1,0:T(8,128)(2,1)S(1)} custom-call(s32[1]{0:T(128)} %bitcast.rank_ref, bf16[192,512]{1,0:T(8,128)(2,1)S(1)} %copy-done.2, bf16[128,256]{1,0:T(8,128)(2,1)S(1)} %collective-permute-done.far3_ref, bf16[192,256]{1,0:T(8,128)(2,1)S(1)} %collective-permute-done.1.far2_ref, bf16[192,512]{1,0:T(8,128)(2,1)S(1)} %collective-permute-done.2.far1_ref, ...), custom_call_target="tpu_custom_call" | custom-call | flops 19327352832 | bytes 6000000 | tf_op jit(solution)/shard_map/attention/pallas_call | solution.py:139
  72.8 0.0 copy-start
  72.9 0.0 copy-start.1
  72.9 28.2 %all_to_all.10.arrived_ref = bf16[8,24,4096]{2,1,0:T(8,128)(2,1)S(1)} all-to-all(bf16[8,24,4096]{2,1,0:T(8,128)(2,1)S(1)} %bitcast.8), channel_id=1, replica_groups=mesh['z'=8,'xh'=2,'core'=2,'y'=4,'xl'=2] {'y','xl'}, dimensions={0} | all-to-all | bytes 3145728 | tf_op jit(solution)/shard_map/all_to_all | solution.py:298
  101.0 1.0 normalize.1
  102.0 24.2 %all_to_all.11 = bf16[8,24,4096]{2,1,0:T(8,128)(2,1)S(1)} all-to-all(bf16[8,24,4096]{2,1,0:T(8,128)(2,1)S(1)} %get-tuple-element.15), channel_id=1, replica_groups=mesh['z'=8,'xh'=2,'core'=2,'y'=4,'xl'=2] {'y','xl'}, dimensions={0} | all-to-all | bytes 3145728 | tf_op jit(solution)/shard_map/all_to_all | solution.py:298
  126.2 0.0 collective-permute-start.3
  126.2 0.1 pad_add_fusion.place_ref
  126.3 3.3 %collective-permute-done.3.theirs_ref = bf16[192,4096]{1,0:T(8,128)(2,1)S(1)} collective-permute-done((bf16[192,4096]{1,0:T(8,128)(2,1)S(1)}, bf16[192,4096]{1,0:T(8,128)(2,1)S(1)}, u32[]{:S(2)}, u32[]{:S(2)}) %collective-permute-start.3) | collective-permute-done | bytes 1572896 | tf_op jit(solution)/shard_map/ppermute | solution.py:288
  129.7 6.2 %product.1 = (f32[192,896]{1,0:T(8,128)S(1)}, bf16[192,896]{1,0:T(8,128)(2,1)S(1)}) custom-call(s32[2]{0:T(128)S(1)} %pad_add_fusion.place_ref, bf16[192,4096]{1,0:T(8,128)(2,1)S(1)} %bitcast.7, bf16[192,4096]{1,0:T(8,128)(2,1)S(1)} %collective-permute-done.3.theirs_ref, bf16[2048,896]{1,0:T(8,128)(2,1)} %all-gather.3.cloned.1.call-done.near_ref, ...), custom_call_target="tpu_custom_call" | custom-call | flops 2818572288 | bytes 10485760 | tf_op jit(solution)/shard_map/product/pallas_call | solution.py:244
  135.8 0.2 collective-permute-start.6
  136.1 1.5 %collective-permute-done.6.back_ref = bf16[192,896]{1,0:T(8,128)(2,1)S(1)} collective-permute-done((bf16[192,896]{1,0:T(8,128)(2,1)S(1)}, bf16[192,896]{1,0:T(8,128)(2,1)S(1)}, u32[]{:S(2)}, u32[]{:S(2)}) %collective-permute-start.6) | collective-permute-done | bytes 344096 | tf_op jit(solution)/shard_map/ppermute | solution.py:288
  137.6 1.5 %finish.1 = bf16[192,896]{1,0:T(8,128)(2,1)} custom-call(s32[2]{0:T(128)S(1)} %pad_add_fusion.place_ref, f32[192,896]{1,0:T(8,128)S(1)} %get-tuple-element.18.us_ref, bf16[192,896]{1,0:T(8,128)(2,1)S(1)} %collective-permute-done.6.back_ref), custom_call_target="tpu_custom_call" | custom-call | tf_op jit(solution)/shard_map/finish/pallas_call | solution.py:277
  (14 shorter events, 0.1 us)
Async XLA Ops:
  7.2 38.4 %copy-start.2 = (bf16[192,512]{1,0:T(8,128)(2,1)S(1)}, bf16[192,512]{1,0:T(8,128)(2,1)}, u32[]{:S(2)}) copy-start(bf16[192,512]{1,0:T(8,128)(2,1)} %q_ref.1) | copy-start | bytes 589828
  7.2 122.5 %all-gather.3.cloned.1.call-start = ((), (), s32[]{:S(2)}) async-start(), calls=%async_computation.2 | async-start | bytes 4128768 | tf_op jit(solution)/shard_map/all_gather | solution.py:340
  9.4 17.9 %copy-start.3 = (bf16[192,512]{1,0:T(8,128)(2,1)S(1)}, bf16[192,512]{1,0:T(8,128)(2,1)}, u32[]{:S(2)}) copy-start(bf16[192,512]{1,0:T(8,128)(2,1)} %get-tuple-element.13.own_ref) | copy-start | bytes 589828
  9.4 19.8 %copy-start.6 = (bf16[192,256]{1,0:T(8,128)(2,1)S(1)}, bf16[192,256]{1,0:T(8,128)(2,1)}, u32[]{:S(2)}) copy-start(bf16[192,256]{1,0:T(8,128)(2,1)} %get-tuple-element.12) | copy-start | bytes 294916
  9.4 24.8 %copy-start.7 = (bf16[128,256]{1,0:T(8,128)(2,1)S(1)}, bf16[128,256]{1,0:T(8,128)(2,1)}, u32[]{:S(2)}) copy-start(bf16[128,256]{1,0:T(8,128)(2,1)} %get-tuple-element.11) | copy-start | bytes 196612
  9.4 1.8 %collective-permute-start.4 = (bf16[128,896]{1,0:T(8,128)(2,1)}, bf16[128,896]{1,0:T(8,128)(2,1)S(1)}, u32[]{:S(2)}, u32[]{:S(2)}) collective-permute-start(bf16[128,896]{1,0:T(8,128)(2,1)} %get-tuple-element.17), channel_id=1, source_target_pairs={{0,8},{8,0},{1,9},{9,1},{2,10},{10,2},{3,11},{11,3},{4,12},{12,4},... | collective-permute-start | bytes 688136 | tf_op jit(solution)/shard_map/ppermute | solution.py:288
  11.2 0.8 copy-start.4
  12.0 117.7 %all-gather.5.cloned.1.call-start = ((), (), s32[]{:S(2)}) async-start(), calls=%async_computation.3 | async-start | bytes 4128768 | tf_op jit(solution)/shard_map/all_gather | solution.py:347
  12.0 14.4 %collective-permute-start.5 = (bf16[256,896]{1,0:T(8,128)(2,1)}, bf16[256,896]{1,0:T(8,128)(2,1)S(1)}, u32[]{:S(2)}, u32[]{:S(2)}) collective-permute-start(bf16[256,896]{1,0:T(8,128)(2,1)} %copy-done.4), channel_id=1, source_target_pairs={{0,16},{16,0},{1,17},{17,1},{2,18},{18,2},{3,19},{19,3},{4,20},{20... | collective-permute-start | bytes 1376264 | tf_op jit(solution)/shard_map/ppermute | solution.py:288
  26.4 0.8 copy-start.5
  27.3 18.3 %collective-permute-start.2 = (bf16[192,512]{1,0:T(8,128)(2,1)S(1)}, bf16[192,512]{1,0:T(8,128)(2,1)S(1)}, u32[]{:S(2)}, u32[]{:S(2)}) collective-permute-start(bf16[192,512]{1,0:T(8,128)(2,1)S(1)} %copy-done.3), channel_id=1, source_target_pairs={{0,8},{8,16},{16,24},{24,32},{32,40},{40,48},{48,56},{56,64},{64,7... | collective-permute-start | bytes 589832 | tf_op jit(solution)/shard_map/ppermute | solution.py:294
  29.2 16.4 %collective-permute-start.1 = (bf16[192,256]{1,0:T(8,128)(2,1)S(1)}, bf16[192,256]{1,0:T(8,128)(2,1)S(1)}, u32[]{:S(2)}, u32[]{:S(2)}) collective-permute-start(bf16[192,256]{1,0:T(8,128)(2,1)S(1)} %copy-done.6), channel_id=1, source_target_pairs={{0,16},{8,24},{16,32},{24,40},{32,48},{40,56},{48,64},{56,72},{64,... | collective-permute-start | bytes 294920 | tf_op jit(solution)/shard_map/ppermute | solution.py:294
  34.2 11.4 %collective-permute-start = (bf16[128,256]{1,0:T(8,128)(2,1)S(1)}, bf16[128,256]{1,0:T(8,128)(2,1)S(1)}, u32[]{:S(2)}, u32[]{:S(2)}) collective-permute-start(bf16[128,256]{1,0:T(8,128)(2,1)S(1)} %copy-done.7), channel_id=1, source_target_pairs={{0,24},{8,32},{16,40},{24,48},{32,56},{40,64},{48,72},{56,80},{64,... | collective-permute-start | bytes 196616 | tf_op jit(solution)/shard_map/ppermute | solution.py:294
  72.8 28.2 %copy-start = (bf16[24,4096]{1,0:T(8,128)(2,1)S(1)}, bf16[24,4096]{1,0:T(8,128)(2,1)}, u32[]{:S(2)}) copy-start(bf16[24,4096]{1,0:T(8,128)(2,1)} %residual_ref.1) | copy-start | bytes 589828
  72.9 28.2 %copy-start.1 = (f32[4096]{0:T(1024)S(1)}, f32[4096]{0:T(1024)}, u32[]{:S(2)}) copy-start(f32[4096]{0:T(1024)} %param.17) | copy-start | bytes 49156
  126.2 3.4 %collective-permute-start.3 = (bf16[192,4096]{1,0:T(8,128)(2,1)S(1)}, bf16[192,4096]{1,0:T(8,128)(2,1)S(1)}, u32[]{:S(2)}, u32[]{:S(2)}) collective-permute-start(bf16[192,4096]{1,0:T(8,128)(2,1)S(1)} %bitcast.6), channel_id=1, source_target_pairs={{0,8},{8,0},{1,9},{9,1},{2,10},{10,2},{3,11},{11,3},{4,12},{12,4},... | collective-permute-start | bytes 4718600 | tf_op jit(solution)/shard_map/ppermute | solution.py:288
  135.8 1.7 %collective-permute-start.6 = (bf16[192,896]{1,0:T(8,128)(2,1)S(1)}, bf16[192,896]{1,0:T(8,128)(2,1)S(1)}, u32[]{:S(2)}, u32[]{:S(2)}) collective-permute-start(bf16[192,896]{1,0:T(8,128)(2,1)S(1)} %get-tuple-element.19), channel_id=1, source_target_pairs={{0,8},{8,0},{1,9},{9,1},{2,10},{10,2},{3,11},{11,3},{4,12},{12,4},... | collective-permute-start | bytes 1032200 | tf_op jit(solution)/shard_map/ppermute | solution.py:288
Sparse Core Ops, SparseCore 0:
  12.1 55.0 all-gather.2
  69.0 49.9 all-gather.4
